TPU v7x, 32 devices: a whole 2x2x4 slice. The times are simulated.
32 devices in a mesh: rep: 2 (over y), grp: 8 (over z, x), tp: 2 (over core).
Axes of the slice: x: 2, y: 2, z: 4, core: 2. Of those that a mesh axis runs over, the one named last changes fastest.
Arguments:
- counts: int32 [16], P(('rep', 'grp')), parts along dimension 0, may hold values from 1 to 8, as said below
- hop_offsets: int32 [128], P(('rep', 'grp')), parts along dimension 0, may hold values from -2 to 2, as said below
- write_pos: int32 [128], P(('rep', 'grp')), parts along dimension 0, may hold values from 0 to 123
- kv_cache: bfloat16 [128, 2, 128, 1024], P(('rep', 'grp'), None, None, 'tp'), parts along dimension 0, may hold values from -27 to 27
- queries: bfloat16 [128, 2, 8192], P(('rep', 'grp'), None, 'tp'), parts along dimension 0, may hold values from -6 to 6
- fresh_kv: bfloat16 [128, 2, 2, 1024], P(('rep', 'grp'), None, None, 'tp'), parts along dimension 0, may hold values from -6 to 6
Outputs:
- new_cache: bfloat16 [128, 2, 128, 1024], P(('rep', 'grp'), None, None, 'tp'), parts along dimension 0
- attended: bfloat16 [128, 2, 8192], P(('rep', 'grp'), None, 'tp'), parts along dimension 0
- served: int32 [16], P('rep'), parts along dimension 0
There are 2 independent parts, one for each index of `rep`. A program takes and returns all parts, laid end to end along the dimension named above; each array names one. Nothing has to cross between parts.
Inputs may be any that keep to these rules, and one draw needn't show every extreme that they name: `counts`: live streams fill a group's first slots; some group holds 8 streams; groups that send hold 8 streams, the others 1 or 2. `hop_offsets`: zero for empty slots and staying streams. A group sends at most one stream with each offset, and no group holds more than 8 streams after the move; offsets -2 and 2 occur.
All inputs are finite; a program needn't handle non-finite values.
Results may differ from a plain program's by a relative error of at most 0.0049.
Values may be sent and summed in bfloat16 or wider, within the bound.
A program may use at most 64 MiB of HBM per device.

v0:
```python
import jax
import jax.numpy as jnp
from jax import lax
from jax.sharding import PartitionSpec as P

HEAD_DIM = 128
SINK = 4
REACH = 2


def for_sending(x):

    def short(part):
        return part.astype(jnp.bfloat16) if part.dtype == jnp.float32 else part

    return jax.tree.map(short, x)


def shifted(block, axis, distance):
    devices = range(lax.axis_size(axis))
    route = [((i - distance) % len(devices), i) for i in devices]
    return lax.ppermute(block, axis, route)


def decode_rows(cache_rows, positions, query_rows, fresh_rows):
    row_count, _, cache_len, kv_width = cache_rows.shape
    group_count = kv_width // HEAD_DIM
    head_count = query_rows.shape[-1] // HEAD_DIM
    group_size = head_count // group_count
    window = cache_len - SINK
    columns = jnp.arange(cache_len, dtype=jnp.int32)
    outputs = []
    current = cache_rows
    for step_index in range(2):
        target = (SINK + (positions + step_index) % window).astype(jnp.int32)
        row_hit = (columns[None, :] == target[:, None])[:, None, :, None]
        current = jnp.where(row_hit, fresh_rows[:, :, step_index][:, :, None, :], current)
        key_rows = current[:, 0].reshape(row_count, cache_len, group_count, HEAD_DIM)
        values = current[:, 1].reshape(row_count, cache_len, group_count, HEAD_DIM)
        query_now = query_rows[:, step_index].reshape(row_count, group_count, group_size, HEAD_DIM)
        scores = jnp.einsum(
            "rgkd,rlgd->rgkl", query_now, key_rows, preferred_element_type=jnp.float32
        ) * HEAD_DIM ** (-0.5)
        weights = jax.nn.softmax(scores, axis=-1).astype(jnp.bfloat16)
        mixed_heads = jnp.einsum(
            "rgkl,rlgd->rgkd", weights, values, preferred_element_type=jnp.float32
        )
        outputs.append(mixed_heads.astype(jnp.bfloat16).reshape(row_count, head_count * HEAD_DIM))
    return (current, jnp.stack(outputs, axis=1))


def per_device(counts, hop_offsets, write_pos, kv_cache, queries, fresh_kv):
    slot_count = kv_cache.shape[0]
    slot_index = jnp.arange(slot_count, dtype=jnp.int32)
    is_live = slot_index < counts[0]
    moving = jnp.where(is_live, hop_offsets, 0)
    staying = is_live & (moving == 0)
    stay_rank = jnp.cumsum(staying.astype(jnp.int32)) - 1
    running = jnp.sum(staying.astype(jnp.int32))
    offsets = [offset for offset in range(-REACH, REACH + 1) if offset != 0]
    arrived = {}
    for direction in (-1, 1):
        row_pieces = []
        pos_pieces = []
        for distance in range(1, REACH + 1):
            chosen = moving == direction * distance
            outgoing_present = jnp.any(chosen)
            picked = jnp.sum(jnp.where(chosen, slot_index, 0))
            rows_out = lax.dynamic_slice_in_dim(kv_cache, picked, 1, 0)
            pos_out = jnp.where(
                outgoing_present, lax.dynamic_slice_in_dim(write_pos, picked, 1, 0), -1
            )
            row_pieces.append(rows_out)
            pos_pieces.append(pos_out)
        carried = (jnp.concatenate(row_pieces, axis=0), jnp.concatenate(pos_pieces, axis=0))
        for distance in range(1, REACH + 1):
            carried = shifted((carried[0], for_sending(carried[1])), "grp", direction)
            arrived[direction * distance] = (carried[0][:1], carried[1][:1])
            carried = (carried[0][1:], carried[1][1:])
    arrived_rows = jnp.concatenate([arrived[offset][0] for offset in offsets], axis=0)
    arrived_pos = jnp.concatenate([arrived[offset][1] for offset in offsets], axis=0)
    present = arrived_pos >= 0
    arrive_rank = running + jnp.cumsum(present.astype(jnp.int32)) - 1
    served_here = running + jnp.sum(present.astype(jnp.int32))
    pool_dest = jnp.concatenate(
        [jnp.where(staying, stay_rank, -1), jnp.where(present, arrive_rank, -1)]
    )
    pool_index = jnp.arange(pool_dest.shape[0], dtype=jnp.int32)
    matches = pool_dest[None, :] == slot_index[:, None]
    filled = jnp.any(matches, axis=1)
    source = jnp.sum(jnp.where(matches, pool_index[None, :], 0), axis=1)
    pool_rows = jnp.concatenate([kv_cache, arrived_rows], axis=0)
    pool_pos = jnp.concatenate([write_pos, arrived_pos], axis=0)
    placed = jnp.take(pool_rows, source, axis=0)
    placed_pos = jnp.take(pool_pos, source)
    result_cache, result_heads = decode_rows(placed, placed_pos, queries, fresh_kv)
    new_cache = jnp.where(filled[:, None, None, None], result_cache, jnp.zeros((), jnp.bfloat16))
    attended = jnp.where(filled[:, None, None], result_heads, jnp.zeros((), jnp.bfloat16))
    served = lax.all_gather(served_here.reshape(1), "grp", axis=0, tiled=True)
    return (new_cache, attended, served)


def solution(mesh):
    return jax.shard_map(
        per_device,
        mesh=mesh,
        in_specs=(
            P(("rep", "grp")),
            P(("rep", "grp")),
            P(("rep", "grp")),
            P(("rep", "grp"), None, None, "tp"),
            P(("rep", "grp"), None, "tp"),
            P(("rep", "grp"), None, None, "tp"),
        ),
        out_specs=(P(("rep", "grp"), None, None, "tp"), P(("rep", "grp"), None, "tp"), P("rep")),
        check_vma=False,
    )
```

profile of v0, /device:TPU:0, one launch (start us, length us, event | category | flops | bytes accessed | tf_op | source)
XLA Modules:
  0.0 102.7 jit_solution(8830002538838391713)
XLA Ops:
  1.3 0.7 convert_bitcast_fusion
  1.9 0.7 fusion.17
  10.6 1.4 %constant_dynamic-slice_fusion.1 = (bf16[1,2,128,512]{3,2,1,0:T(8,128)(2,1)S(1)}, bf16[1,2,128,512]{3,2,1,0:T(8,128)(2,1)S(1)}, bf16[1,2,128,512]{3,2,1,0:T(8,128)(2,1)S(1)}, bf16[1,2,128,512]{3,2,1,0:T(8,128)(2,1)S(1)}) fusion(bf16[8,2,128,512]{3,2,1,0:T(8,128)(2,1)} %param.9, s32[]{:T(128)S(6)} %select_n.154, s32[]{:T(128)S(6)} %select_n.150, ...), kind=kLoop, calls=%fused_computation.62 | loop fusion | bytes 2097168 | tf_op jit(solution)/shard_map/dynamic_slice | solution.py:69
  12.1 0.9 pad_maximum_fusion
  12.9 6.0 %collective-permute-start.4 = (bf16[2,2,128,512]{3,2,1,0:T(8,128)(2,1)}, bf16[2,2,128,512]{3,2,1,0:T(8,128)(2,1)}, u32[]{:S(2)}, u32[]{:S(2)}) collective-permute-start(bf16[2,2,128,512]{3,2,1,0:T(8,128)(2,1)} %pad_maximum_fusion), channel_id=1, source_target_pairs={{2,0},{4,2},{6,4},{8,6},{10,8},{12,10},{14,12},{0,14},{3,1},{5,3},... | collective-permute-start | bytes 1572872 | tf_op jit(solution)/shard_map/ppermute | solution.py:22
  18.9 0.8 pad_maximum_fusion.1
  19.8 0.7 compare_reduce_fusion.3
  20.5 0.7 fusion.28
  23.8 4.7 %collective-permute-start = (s32[2]{0:T(128)S(1)}, s32[2]{0:T(128)S(1)}, u32[]{:S(2)}, u32[]{:S(2)}) collective-permute-start(s32[2]{0:T(128)S(1)} %pad_add_fusion), channel_id=1, source_target_pairs={{2,0},{4,2},{6,4},{8,6},{10,8},{12,10},{14,12},{0,14},{3,1},{5,3},... | collective-permute-start | bytes 32 | tf_op jit(solution)/shard_map/ppermute | solution.py:22
  32.0 0.6 copy.28
  32.6 0.6 slice_reduce_fusion.1
  33.1 0.6 bitcast_select_fusion
  33.7 0.7 dynamic-slice
  34.4 4.9 %collective-permute-done = s32[2]{0:T(128)S(1)} collective-permute-done((s32[2]{0:T(128)S(1)}, s32[2]{0:T(128)S(1)}, u32[]{:S(2)}, u32[]{:S(2)}) %collective-permute-start) | collective-permute-done | bytes 40 | tf_op jit(solution)/shard_map/ppermute | solution.py:22
  39.3 0.6 fusion.27
  40.0 2.9 %collective-permute-start.1 = (s32[1]{0:T(128)}, s32[1]{0:T(128)}, u32[]{:S(2)}, u32[]{:S(2)}) collective-permute-start(s32[1]{0:T(128)} %get-tuple-element.37), channel_id=1, source_target_pairs={{2,0},{4,2},{6,4},{8,6},{10,8},{12,10},{14,12},{0,14},{3,1},{5,3},... | collective-permute-start | bytes 20 | tf_op jit(solution)/shard_map/ppermute | solution.py:22
  42.9 0.6 fusion.29
  43.5 0.7 collective-permute-done.1
  44.2 5.7 %collective-permute-done.3 = s32[1]{0:T(128)} collective-permute-done((s32[1]{0:T(128)}, s32[1]{0:T(128)}, u32[]{:S(2)}, u32[]{:S(2)}) %collective-permute-start.3) | collective-permute-done | bytes 36 | tf_op jit(solution)/shard_map/ppermute | solution.py:22
  49.9 2.6 %compare_convert_fusion = s32[4,1]{0,1:T(1,128)S(1)} fusion(s32[1,1]{0,1:T(1,128)} %bitcast.10, s32[1,1]{0,1:T(1,128)} %bitcast.9, s32[1,1]{0,1:T(1,128)} %bitcast.8, s32[1,1]{0,1:T(1,128)} %bitcast.7), kind=kLoop, calls=%fused_computation.48 | loop fusion | flops 20 | bytes 32 | tf_op jit(solution)/shard_map/convert_element_type | solution.py:83
  52.7 3.3 %fusion.19 = (s32[]{:T(128)}, s32[4]{0:T(128)S(1)}) fusion(s32[1]{0:T(128)} %collective-permute-done.3, s32[1]{0:T(128)} %get-tuple-element.43, s32[1]{0:T(128)} %get-tuple-element.38, s32[1]{0:T(128)} %collective-permute-done.1), kind=kLoop, calls=%fused_computation.69 | loop fusion | flops 23 | bytes 36 | tf_op jit(solution)/shard_map/reduce_sum | solution.py:84
  56.0 0.5 compare_select_fusion.2
  56.8 2.7 %concatenate.51 = s32[12]{0:T(128)S(1)} concatenate(s32[8]{0:T(128)S(1)} %copy-done.4, s32[1]{0:T(128)} %collective-permute-done.1, s32[1]{0:T(128)} %get-tuple-element.38, s32[1]{0:T(128)} %get-tuple-element.43, s32[1]{0:T(128)} %collective-permute-done.3), dimensions={0} | concatenate | bytes 96 | tf_op jit(solution)/shard_map/concatenate | solution.py:93
  59.5 0.6 gather_fusion
  60.1 0.6 fusion.20
  60.7 1.7 %slice.68 = bf16[1,2,128,512]{3,2,1,0:T(8,128)(2,1)} slice(bf16[2,2,128,512]{3,2,1,0:T(8,128)(2,1)} %collective-permute-done.4), slice={[1:2], [0:2], [0:128], [0:512]} | slice | bytes 524288 | tf_op jit(solution)/shard_map/slice | solution.py:79
  62.4 1.2 %fusion.21 = s32[8]{0:T(128)} fusion(pred[8]{0:T(512)(128)(4,1)S(1)} %get-tuple-element.19, s32[8]{0:T(128)} %copy-done.9), kind=kLoop, calls=%fused_computation.71 | loop fusion | flops 64 | bytes 72 | tf_op jit(solution)/shard_map/add | solution.py:35
  64.8 0.5 broadcast_in_dim.111
  65.3 1.8 %dynamic-update-slice = s32[8]{0:T(128)} dynamic-update-slice(s32[8]{0:T(128)} %broadcast_in_dim.111, s32[1]{0:T(128)} %bitcast.22, u32[]{:T(128)} %bitcast.23) | dynamic-update-slice | bytes 12
  67.0 1.3 %iota_compare_fusion = pred[8,128]{1,0:T(8,128)(4,1)} fusion(s32[8]{0:T(128)} %fusion.21), kind=kLoop, calls=%fused_computation.38 | loop fusion | flops 1024 | bytes 1056 | tf_op jit(solution)/shard_map/eq | solution.py:36
  68.3 0.7 collective-permute-done.5
  69.0 1.0 slice_dynamic-update-slice_fusion.1
  70.0 1.8 %fusion.25 = (bf16[1,2,128,512]{3,2,1,0:T(8,128)(2,1)}, bf16[12,2,128,512]{3,2,1,0:T(8,128)(2,1)S(1)}) fusion(bf16[2,2,128,512]{3,2,1,0:T(8,128)(2,1)} %collective-permute-done.6, bf16[12,2,128,512]{3,2,1,0:T(8,128)(2,1)S(1)} %slice_dynamic-update-slice_fusion.1), kind=kLoop, calls=%fused_computation.83 | loop fusion | bytes 1048576 | tf_op jit(solution)/shard_map/slice | solution.py:79
  71.8 1.3 %collective-permute-start.7 = (bf16[1,2,128,512]{3,2,1,0:T(8,128)(2,1)}, bf16[1,2,128,512]{3,2,1,0:T(8,128)(2,1)S(1)}, u32[]{:S(2)}, u32[]{:S(2)}) collective-permute-start(bf16[1,2,128,512]{3,2,1,0:T(8,128)(2,1)} %get-tuple-element.31), channel_id=1, source_target_pairs={{14,0},{0,2},{2,4},{4,6},{6,8},{8,10},{10,12},{12,14},{15,1},{1,3}... | collective-permute-start | bytes 786440 | tf_op jit(solution)/shard_map/ppermute | solution.py:22
  73.1 0.7 fusion.14
  73.8 10.6 %all-reduce = s32[8]{0:T(128)} all-reduce(s32[8]{0:T(128)} %dynamic-update-slice), channel_id=1, replica_groups=mesh['rep'=2,'grp'=8,'tp'=2] {'grp'}, use_global_device_ids=true, to_apply=%add | all-reduce | flops 8 | bytes 64
  84.4 1.3 %iota_compare_fusion.1 = pred[8,128]{1,0:T(8,128)(4,1)} fusion(s32[8]{0:T(128)} %get-tuple-element.18), kind=kLoop, calls=%fused_computation.40 | loop fusion | flops 1024 | bytes 1056 | tf_op jit(solution)/shard_map/eq | solution.py:36
  85.8 2.1 %gather_fusion.1 = bf16[8,2,128,512]{3,2,1,0:T(8,128)(2,1)} fusion(bf16[12,2,128,512]{3,2,1,0:T(8,128)(2,1)S(1)} %constant_dynamic-update-slice_fusion, s32[1024]{0:T(1024)} %copy-done.5), kind=kCustom, calls=%fused_computation.1 | custom fusion | bytes 4194336 | tf_op jit(solution)/shard_map/jit(_take)/gather | solution.py:94
  87.9 2.9 %broadcast_select_fusion = (bf16[8,2,128,512]{3,2,1,0:T(8,128)(2,1)}, bf16[8,2,128,512]{3,2,1,0:T(8,128)(2,1)S(1)}, bf16[8,2,128,512]{3,2,1,0:T(8,128)(2,1)S(1)}) fusion(pred[8]{0:T(512)(128)(4,1)S(1)} %copy-done.6, bf16[8,2,512]{2,1,0:T(2,128)(2,1)S(1)} %copy.26, pred[8,128]{1,0:T(8,128)(4,1)S(1)} %copy-done.11, bf16[8,2,128,512]{3,2,1,0:T(8,128)(2,1)} %gather_fusion.1, ...), kind=kLoop, calls=%fused_computation.5 | loop fusion | flops 4194304 | bytes 8423440 | tf_op jit(solution)/shard_map/jit(_where)/select_n | solution.py:97
  90.8 1.6 %fusion.23 = (bf16[8,1,128,512]{3,2,1,0:T(8,128)(2,1)}, bf16[8,1,128,512]{3,2,1,0:T(8,128)(2,1)}) fusion(bf16[8,2,128,512]{3,2,1,0:T(8,128)(2,1)S(1)} %get-tuple-element.17), kind=kLoop, calls=%fused_computation.81 | loop fusion | bytes 4194304 | tf_op jit(solution)/shard_map/slice | solution.py:38
  92.4 1.6 %copy.29 = bf16[8,1,128,512]{2,3,0,1:T(8,128)(2,1)S(1)} copy(bf16[8,1,128,512]{3,2,1,0:T(8,128)(2,1)} %get-tuple-element.23) | data formatting | bytes 2097152 | tf_op jit(solution)/shard_map/slice | solution.py:38
  94.6 1.6 %copy.31 = bf16[8,1,128,512]{2,3,0,1:T(8,128)(2,1)S(1)} copy(bf16[8,1,128,512]{3,2,1,0:T(8,128)(2,1)} %get-tuple-element.24) | data formatting | bytes 2097152 | tf_op jit(solution)/shard_map/slice | solution.py:39
  96.2 0.7 convolution_convert_fusion.1
  96.9 1.2 %fusion.24 = (bf16[8,1,128,512]{3,2,1,0:T(8,128)(2,1)}, bf16[8,1,128,512]{3,2,1,0:T(8,128)(2,1)S(1)}) fusion(bf16[8,2,128,512]{3,2,1,0:T(8,128)(2,1)S(1)} %get-tuple-element.16), kind=kLoop, calls=%fused_computation.82 | loop fusion | bytes 4194304 | tf_op jit(solution)/shard_map/slice | solution.py:38
  98.1 1.6 %copy.33 = bf16[8,1,128,512]{2,3,0,1:T(8,128)(2,1)S(1)} copy(bf16[8,1,128,512]{3,2,1,0:T(8,128)(2,1)} %get-tuple-element.25) | data formatting | bytes 2097152 | tf_op jit(solution)/shard_map/slice | solution.py:38
  100.3 0.7 copy.35
  101.0 0.7 convolution_convert_fusion
  101.7 1.0 broadcast_select_fusion.2
  (58 shorter events, 2.7 us)
Async XLA Ops:
  10.6 9.9 %copy-start.4 = (s32[8]{0:T(128)S(1)}, s32[8]{0:T(128)}, u32[]{:S(2)}) copy-start(s32[8]{0:T(128)} %param.8) | copy-start | bytes 100
  10.6 20.6 %copy-start = (bf16[8,2,128,512]{3,2,1,0:T(8,128)(2,1)S(1)}, bf16[8,2,128,512]{3,2,1,0:T(8,128)(2,1)}, u32[]{:S(2)}) copy-start(bf16[8,2,128,512]{3,2,1,0:T(8,128)(2,1)} %param.9) | copy-start | bytes 6291460
  12.9 47.8 %collective-permute-start.4 = (bf16[2,2,128,512]{3,2,1,0:T(8,128)(2,1)}, bf16[2,2,128,512]{3,2,1,0:T(8,128)(2,1)}, u32[]{:S(2)}, u32[]{:S(2)}) collective-permute-start(bf16[2,2,128,512]{3,2,1,0:T(8,128)(2,1)} %pad_maximum_fusion), channel_id=1, source_target_pairs={{2,0},{4,2},{6,4},{8,6},{10,8},{12,10},{14,12},{0,14},{3,1},{5,3},... | collective-permute-start | bytes 1572872 | tf_op jit(solution)/shard_map/ppermute | solution.py:22
  19.8 50.2 %collective-permute-start.6 = (bf16[2,2,128,512]{3,2,1,0:T(8,128)(2,1)}, bf16[2,2,128,512]{3,2,1,0:T(8,128)(2,1)}, u32[]{:S(2)}, u32[]{:S(2)}) collective-permute-start(bf16[2,2,128,512]{3,2,1,0:T(8,128)(2,1)} %pad_maximum_fusion.1), channel_id=1, source_target_pairs={{14,0},{0,2},{2,4},{4,6},{6,8},{8,10},{10,12},{12,14},{15,1},{1,3}... | collective-permute-start | bytes 1572872 | tf_op jit(solution)/shard_map/ppermute | solution.py:22
  23.8 15.5 %collective-permute-start = (s32[2]{0:T(128)S(1)}, s32[2]{0:T(128)S(1)}, u32[]{:S(2)}, u32[]{:S(2)}) collective-permute-start(s32[2]{0:T(128)S(1)} %pad_add_fusion), channel_id=1, source_target_pairs={{2,0},{4,2},{6,4},{8,6},{10,8},{12,10},{14,12},{0,14},{3,1},{5,3},... | collective-permute-start | bytes 32 | tf_op jit(solution)/shard_map/ppermute | solution.py:22
  31.1 0.8 copy-start.2
  31.1 1.5 %copy-start.1 = (bf16[8,2,4096]{2,1,0:T(2,128)(2,1)S(1)}, bf16[8,2,4096]{2,1,0:T(2,128)(2,1)}, u32[]{:S(2)}) copy-start(bf16[8,2,4096]{2,1,0:T(2,128)(2,1)} %param.10) | copy-start | bytes 393220
  31.1 2.6 %copy-start.12 = (u32[32]{0:T(128)S(1)}, u32[32]{0:T(128)}, u32[]{:S(2)}) copy-start(u32[32]{0:T(128)} %constant.89) | copy-start | bytes 388
  31.1 11.7 %collective-permute-start.2 = (s32[2]{0:T(128)S(1)}, s32[2]{0:T(128)S(1)}, u32[]{:S(2)}, u32[]{:S(2)}) collective-permute-start(s32[2]{0:T(128)S(1)} %pad_add_fusion.1), channel_id=1, source_target_pairs={{14,0},{0,2},{2,4},{4,6},{6,8},{8,10},{10,12},{12,14},{15,1},{1,3}... | collective-permute-start | bytes 32 | tf_op jit(solution)/shard_map/ppermute | solution.py:22
  40.0 4.2 %collective-permute-start.1 = (s32[1]{0:T(128)}, s32[1]{0:T(128)}, u32[]{:S(2)}, u32[]{:S(2)}) collective-permute-start(s32[1]{0:T(128)} %get-tuple-element.37), channel_id=1, source_target_pairs={{2,0},{4,2},{6,4},{8,6},{10,8},{12,10},{14,12},{0,14},{3,1},{5,3},... | collective-permute-start | bytes 20 | tf_op jit(solution)/shard_map/ppermute | solution.py:22
  43.5 6.4 %collective-permute-start.3 = (s32[1]{0:T(128)}, s32[1]{0:T(128)}, u32[]{:S(2)}, u32[]{:S(2)}) collective-permute-start(s32[1]{0:T(128)} %get-tuple-element.44), channel_id=1, source_target_pairs={{14,0},{0,2},{2,4},{4,6},{6,8},{8,10},{10,12},{12,14},{15,1},{1,3}... | collective-permute-start | bytes 20 | tf_op jit(solution)/shard_map/ppermute | solution.py:22
  56.7 4.1 %copy-start.13 = (s32[12]{0:T(128)}, s32[12]{0:T(128)S(1)}, u32[]{:S(2)}) copy-start(s32[12]{0:T(128)S(1)} %pad_add_fusion.3) | copy-start | bytes 148
  59.4 1.3 %copy-start.5 = (s32[1024]{0:T(1024)}, s32[1024]{0:T(1024)S(1)}, u32[]{:S(2)}) copy-start(s32[1024]{0:T(1024)S(1)} %pad_clamp_fusion) | copy-start | bytes 12292
  60.1 0.6 copy-start.9
  60.7 1.7 %copy-start.7 = (pred[8]{0:T(512)(128)(4,1)}, pred[8]{0:T(512)(128)(4,1)S(1)}, u32[]{:S(2)}) copy-start(pred[8]{0:T(512)(128)(4,1)S(1)} %get-tuple-element.19) | copy-start | bytes 28
  62.4 6.6 %collective-permute-start.5 = (bf16[1,2,128,512]{3,2,1,0:T(8,128)(2,1)}, bf16[1,2,128,512]{3,2,1,0:T(8,128)(2,1)S(1)}, u32[]{:S(2)}, u32[]{:S(2)}) collective-permute-start(bf16[1,2,128,512]{3,2,1,0:T(8,128)(2,1)} %slice.68), channel_id=1, source_target_pairs={{2,0},{4,2},{6,4},{8,6},{10,8},{12,10},{14,12},{0,14},{3,1},{5,3},... | collective-permute-start | bytes 786440 | tf_op jit(solution)/shard_map/ppermute | solution.py:22
  67.0 6.1 %copy-start.14 = (s32[12]{0:T(128)S(1)}, s32[12]{0:T(128)}, u32[]{:S(2)}) copy-start(s32[12]{0:T(128)} %copy-done.13) | copy-start | bytes 148
  71.8 13.9 %collective-permute-start.7 = (bf16[1,2,128,512]{3,2,1,0:T(8,128)(2,1)}, bf16[1,2,128,512]{3,2,1,0:T(8,128)(2,1)S(1)}, u32[]{:S(2)}, u32[]{:S(2)}) collective-permute-start(bf16[1,2,128,512]{3,2,1,0:T(8,128)(2,1)} %get-tuple-element.31), channel_id=1, source_target_pairs={{14,0},{0,2},{2,4},{4,6},{6,8},{8,10},{10,12},{12,14},{15,1},{1,3}... | collective-permute-start | bytes 786440 | tf_op jit(solution)/shard_map/ppermute | solution.py:22
  85.7 2.2 %copy-start.3 = (bf16[8,2,512]{2,1,0:T(2,128)(2,1)S(1)}, bf16[8,2,512]{2,1,0:T(2,128)(2,1)}, u32[]{:S(2)}) copy-start(bf16[8,2,512]{2,1,0:T(2,128)(2,1)} %copy.28) | copy-start | bytes 49156
  85.7 2.2 %copy-start.6 = (pred[8]{0:T(512)(128)(4,1)S(1)}, pred[8]{0:T(512)(128)(4,1)}, u32[]{:S(2)}) copy-start(pred[8]{0:T(512)(128)(4,1)} %fusion.14) | copy-start | bytes 28
  85.8 2.2 %copy-start.8 = (pred[8]{0:T(512)(128)(4,1)S(1)}, pred[8]{0:T(512)(128)(4,1)}, u32[]{:S(2)}) copy-start(pred[8]{0:T(512)(128)(4,1)} %copy-done.7) | copy-start | bytes 28
  85.8 2.2 %copy-start.10 = (pred[8,128]{1,0:T(8,128)(4,1)S(1)}, pred[8,128]{1,0:T(8,128)(4,1)}, u32[]{:S(2)}) copy-start(pred[8,128]{1,0:T(8,128)(4,1)} %iota_compare_fusion) | copy-start | bytes 3076
  85.8 2.2 %copy-start.11 = (pred[8,128]{1,0:T(8,128)(4,1)S(1)}, pred[8,128]{1,0:T(8,128)(4,1)}, u32[]{:S(2)}) copy-start(pred[8,128]{1,0:T(8,128)(4,1)} %iota_compare_fusion.1) | copy-start | bytes 3076
where the time goes:
time: 103 us
  local copies, waits for them, and re-layouts  26.3 us (26%)
  other arithmetic  21 us (20%)
  between operations  15.6 us (15%)
  starting transfers between devices  15 us (15%)
  waiting for transfers between devices  12.1 us (12%)
  blocking collectives  10.6 us (10%)
  matrix products  2.14 us (2%)
    ppermute x8, starting transfers between devices, shifted(): return lax.ppermute(block, axis, route)  15 us
    ppermute x8, waiting for transfers between devices, shifted(): return lax.ppermute(block, axis, route)  12.1 us
    unnamed x1, blocking collectives  10.6 us
    slice x4, local copies, waits for them, and re-layouts, decode_rows(): current[:, 0].reshape(row_count, cache_len, group_count, HEAD_DIM)  5.96 us
    slice x3, local copies, waits for them, and re-layouts, per_device(): carried = (carried[0][1:], carried[1][1:])  4.11 us
    unnamed x35, local copies, waits for them, and re-layouts  3.98 us
    reduce_sum x1, other arithmetic, per_device(): served_here = running + jnp.sum(present.astype(jnp.int32))  3.3 us
    select_n x1, other arithmetic, per_device(): jnp.where(filled[:, None, None, None], result_cache, jnp.zeros((), jnp.bf...  2.85 us
  transfers between devices with their start and end apart: 8, of which 4 were waited for; matrix products, arithmetic and copies ran while one was open for 26% of the time, Pallas kernels for 0%

commit v1 on v0

v1 whole, which is shorter than its diff:
```python
import functools

import jax
import jax.numpy as jnp
from jax import lax
from jax.experimental import pallas as pl
from jax.experimental.pallas import tpu as pltpu
from jax.sharding import PartitionSpec as P

HEAD_DIM = 128
SINK = 4
OFFSETS = (-2, -1, 1, 2)
PACK = 16


def exchange_kernel(n, counts_ref, hops_ref, pos_ref, kv_ref, arrived_ref, table_ref,
                    staged, meta, send_sem, recv_sem, meta_send, meta_recv, own_sem):
    me = lax.axis_index("grp")
    slots = kv_ref.shape[0]
    barrier = pltpu.get_barrier_semaphore()

    @pl.loop(1, n)
    def _(k):
        pl.semaphore_signal(barrier, inc=1, device_id={"grp": lax.rem(me + k, n)})

    live = counts_ref[0]
    stay = jnp.int32(0)
    picked = [jnp.int32(0) for _ in OFFSETS]
    position = [jnp.int32(-1) for _ in OFFSETS]
    for s in range(slots):
        hop = jnp.where(s < live, hops_ref[s], 0)
        stay = stay + jnp.where((s < live) & (hop == 0), 1, 0)
        for i, offset in enumerate(OFFSETS):
            hit = hop == offset
            picked[i] = jnp.where(hit, s, picked[i])
            position[i] = jnp.where(hit, pos_ref[s], position[i])
    lane = lax.broadcasted_iota(jnp.int32, (1, 128), 1)
    row = jnp.where(lane == 0, stay, 0)
    for i in range(len(OFFSETS)):
        row = jnp.where(lane == 1 + i, position[i], row)
    meta[...] = row
    for i in range(len(OFFSETS)):
        staged[i] = kv_ref[picked[i]]

    pl.semaphore_wait(barrier, n - 1)

    def meta_copy(k):
        return pltpu.make_async_remote_copy(
            src_ref=meta, dst_ref=table_ref.at[me], send_sem=meta_send.at[k],
            recv_sem=meta_recv.at[k], device_id={"grp": lax.rem(me + k, n)})

    copies = []
    for i, offset in enumerate(OFFSETS):
        copies.append(pltpu.make_async_remote_copy(
            src_ref=staged.at[i], dst_ref=arrived_ref.at[i], send_sem=send_sem.at[i],
            recv_sem=recv_sem.at[i], device_id={"grp": lax.rem(me + offset + n, n)}))

    @pl.loop(1, n)
    def _(k):
        meta_copy(k).start()

    for i in (0, 3, 1, 2):
        copies[i].start()
    own = pltpu.make_async_copy(meta, table_ref.at[me], own_sem)
    own.start()
    own.wait()

    @pl.loop(1, n)
    def _(k):
        meta_copy(k).wait()

    for copy in copies:
        copy.wait()


def exchange(n, counts, hops, pos, kv):
    many = len(OFFSETS)
    smem = pl.BlockSpec(memory_space=pltpu.SMEM)
    vmem = pl.BlockSpec(memory_space=pltpu.VMEM)
    hbm = pl.BlockSpec(memory_space=pl.ANY)
    dma = pltpu.SemaphoreType.DMA
    return pl.pallas_call(
        functools.partial(exchange_kernel, n),
        out_shape=(jax.ShapeDtypeStruct((many,) + kv.shape[1:], kv.dtype),
                   jax.ShapeDtypeStruct((n, 1, 128), jnp.int32)),
        in_specs=[smem, smem, smem, vmem],
        out_specs=(hbm, hbm),
        scratch_shapes=[pltpu.VMEM((many,) + kv.shape[1:], kv.dtype),
                        pltpu.VMEM((1, 128), jnp.int32),
                        dma((many,)), dma((many,)), dma((n,)), dma((n,)), dma(())],
        compiler_params=pltpu.CompilerParams(collective_id=0, has_side_effects=True),
        name="exchange",
    )(counts, hops, pos, kv)


def decode_kernel(n, counts_ref, hops_ref, pos_ref, table_ref, kv_ref, arrived_ref, q_ref, fresh_ref,
                  out_ref, heads_ref, served_ref,
                  buf, zeros, q_rows, o_rows, place_pos, in_sem, out_sem):
    me = lax.axis_index("grp")
    slots, _, cache_len, width = kv_ref.shape
    kv_heads = width // HEAD_DIM
    heads = q_ref.shape[-1] // HEAD_DIM
    rows = 2 * heads // kv_heads
    window = cache_len - SINK

    live = counts_ref[0]
    filled = jnp.int32(0)
    for s in range(slots):
        stays = (s < live) & (hops_ref[s] == 0)

        @pl.when(stays)
        def _(s=s, at=filled):
            place_pos[at] = pos_ref[s]
            pltpu.make_async_copy(kv_ref.at[s], buf.at[at], in_sem.at[at]).start()

        filled = filled + jnp.where(stays, 1, 0)
    for i, offset in enumerate(OFFSETS):
        position = table_ref[lax.rem(me - offset + n, n), 0, 1 + i]
        present = position >= 0

        @pl.when(present)
        def _(i=i, at=filled, position=position):
            place_pos[at] = position
            pltpu.make_async_copy(arrived_ref.at[i], buf.at[at], in_sem.at[at]).start()

        filled = filled + jnp.where(present, 1, 0)

    zeros[...] = jnp.zeros_like(zeros)

    @pl.loop(0, n)
    def _(g):
        total = table_ref[g, 0, 0]
        for i, offset in enumerate(OFFSETS):
            total = total + jnp.where(table_ref[lax.rem(g - offset + n, n), 0, 1 + i] >= 0, 1, 0)
        served_ref[g] = total

    @pl.loop(filled, slots)
    def _(j):
        heads_ref[j] = jnp.zeros(heads_ref.shape[1:], heads_ref.dtype)
        pltpu.make_async_copy(zeros, out_ref.at[j], out_sem.at[j]).start()

    column = lax.broadcasted_iota(jnp.int32, (rows, cache_len), 1)
    first = lax.rem(lax.broadcasted_iota(jnp.int32, (rows, cache_len), 0), 2) == 0
    sub = lax.broadcasted_iota(jnp.int32, (PACK, width), 0)

    @pl.loop(0, filled)
    def _(j):
        q = q_ref[j].astype(jnp.float32)
        for h in range(heads):
            q_rows[2 * h:2 * h + 2] = q[:, h * HEAD_DIM:(h + 1) * HEAD_DIM]
        pltpu.make_async_copy(kv_ref.at[0], buf.at[j], in_sem.at[j]).wait()
        position = place_pos[j]
        target = [SINK + lax.rem(position + t, window) for t in range(2)]
        old = []
        for c in range(2):
            fresh = fresh_ref[j, c].astype(jnp.float32)
            for t in range(2):
                base = pl.multiple_of((target[t] // PACK) * PACK, PACK)
                block = buf[j, c, pl.ds(base, PACK), :].astype(jnp.float32)
                hit = sub + base == target[t]
                if t == 1:
                    old.append(jnp.sum(jnp.where(hit, block, 0.0), axis=0, keepdims=True))
                buf[j, c, pl.ds(base, PACK), :] = jnp.where(hit, fresh[t:t + 1], block).astype(buf.dtype)
        pltpu.make_async_copy(buf.at[j], out_ref.at[j], out_sem.at[j]).start()
        stale = first & (column == target[1])
        for g in range(kv_heads):
            lanes = slice(g * HEAD_DIM, (g + 1) * HEAD_DIM)
            query = q_rows[g * rows:(g + 1) * rows]
            keys = buf[j, 0, :, lanes]
            values = buf[j, 1, :, lanes]
            scores = lax.dot_general(query.astype(jnp.bfloat16), keys, (((1,), (1,)), ((), ())),
                                     preferred_element_type=jnp.float32)
            before = jnp.sum(query * old[0][:, lanes], axis=1, keepdims=True)
            scores = jnp.where(stale, before, scores) * HEAD_DIM ** -0.5
            raised = jnp.exp(scores - jnp.max(scores, axis=1, keepdims=True))
            weights = (raised / jnp.sum(raised, axis=1, keepdims=True)).astype(jnp.bfloat16)
            wide = weights.astype(jnp.float32)
            kept = jnp.where(stale, 0.0, wide).astype(jnp.bfloat16)
            stale_weight = jnp.sum(jnp.where(stale, wide, 0.0), axis=1, keepdims=True)
            mixed = lax.dot_general(kept, values, (((1,), (0,)), ((), ())),
                                    preferred_element_type=jnp.float32)
            o_rows[g * rows:(g + 1) * rows] = mixed + stale_weight * old[1][:, lanes]
        for h in range(heads):
            heads_ref[j, :, h * HEAD_DIM:(h + 1) * HEAD_DIM] = o_rows[2 * h:2 * h + 2].astype(heads_ref.dtype)

    @pl.loop(0, slots)
    def _(j):
        pltpu.make_async_copy(zeros, out_ref.at[j], out_sem.at[j]).wait()


def decode(n, counts, hops, pos, table, kv, arrived, queries, fresh):
    smem = pl.BlockSpec(memory_space=pltpu.SMEM)
    vmem = pl.BlockSpec(memory_space=pltpu.VMEM)
    hbm = pl.BlockSpec(memory_space=pl.ANY)
    dma = pltpu.SemaphoreType.DMA
    slots = kv.shape[0]
    heads = queries.shape[-1] // HEAD_DIM
    return pl.pallas_call(
        functools.partial(decode_kernel, n),
        out_shape=(jax.ShapeDtypeStruct(kv.shape, kv.dtype),
                   jax.ShapeDtypeStruct(queries.shape, queries.dtype),
                   jax.ShapeDtypeStruct((n,), jnp.int32)),
        in_specs=[smem, smem, smem, smem, hbm, hbm, vmem, vmem],
        out_specs=(hbm, vmem, smem),
        scratch_shapes=[pltpu.VMEM(kv.shape, kv.dtype),
                        pltpu.VMEM(kv.shape[1:], kv.dtype),
                        pltpu.VMEM((2 * heads, HEAD_DIM), jnp.float32),
                        pltpu.VMEM((2 * heads, HEAD_DIM), jnp.float32),
                        pltpu.SMEM((slots,), jnp.int32),
                        dma((slots,)), dma((slots,))],
        name="decode",
    )(counts, hops, pos, table, kv, arrived, queries, fresh)


def solution(mesh):
    n = mesh.shape["grp"]

    def per_device(counts, hop_offsets, write_pos, kv_cache, queries, fresh_kv):
        arrived, table = exchange(n, counts, hop_offsets, write_pos, kv_cache)
        return decode(n, counts, hop_offsets, write_pos, table, kv_cache, arrived, queries, fresh_kv)

    return jax.shard_map(
        per_device,
        mesh=mesh,
        in_specs=(
            P(("rep", "grp")),
            P(("rep", "grp")),
            P(("rep", "grp")),
            P(("rep", "grp"), None, None, "tp"),
            P(("rep", "grp"), None, "tp"),
            P(("rep", "grp"), None, None, "tp"),
        ),
        out_specs=(P(("rep", "grp"), None, None, "tp"), P(("rep", "grp"), None, "tp"), P("rep")),
        check_vma=False,
    )
```

time: 103 us -> 35.9 us (0.35)
  Pallas kernels: 0 us -> 34.5 us
  local copies, waits for them, and re-layouts: 26.3 us -> 0 us
  other arithmetic: 21 us -> 0 us
  starting transfers between devices: 15 us -> 0 us
  between operations: 15.6 us -> 1.28 us
  waiting for transfers between devices: 12.1 us -> 0 us
  blocking collectives: 10.6 us -> 0 us
  matrix products: 2.14 us -> 0 us
    pallas_call x0 -> x2, Pallas kernels: none -> 34.5 us  [the longest x1 26 us: exchange(): pl.pallas_call(functools.partial(exchange_kernel, n), out_shape=(jax.Shap...]
    ppermute x8 -> x0, starting transfers between devices: 15 us -> none  [shifted(): return lax.ppermute(block, axis, route)]
    slice x12 -> x0, local copies, waits for them, and re-layouts: 13.6 us -> none  [the longest x4 5.96 us: decode_rows(): current[:, 0].reshape(row_count, cache_len, group_count, HEAD_DIM)]
    ppermute x8 -> x0, waiting for transfers between devices: 12.1 us -> none  [shifted(): return lax.ppermute(block, axis, route)]
    unnamed x1 -> x0, blocking collectives: 10.6 us -> none
    select_n x5 -> x0, other arithmetic: 4.99 us -> none  [the longest x1 2.85 us: per_device(): jnp.where(filled[:, None, None, None], result_cache, jnp.zeros((), jnp.bf...]
    reduce_sum x3 -> x0, other arithmetic: 4.16 us -> none  [the longest x1 3.3 us: per_device(): served_here = running + jnp.sum(present.astype(jnp.int32))]
    unnamed x35 -> x0, local copies, waits for them, and re-layouts: 3.98 us -> none
  transfers between devices with their start and end apart: 8 -> 0, of which waited for: 4 -> 0; matrix products, arithmetic and copies ran while one was open for 26% -> 0% of each run, Pallas kernels for 0% -> 0%
where the time goes in v1:
time: 35.9 us; the launch traced here: 35.7 us
  Pallas kernels  34.5 us (96%)
  between operations  1.28 us (4%)
    pallas_call x1, Pallas kernels, exchange(): pl.pallas_call(functools.partial(exchange_kernel, n), out_shape=(jax.Shap...  26 us
    pallas_call x1, Pallas kernels, decode(): pl.pallas_call(functools.partial(decode_kernel, n), out_shape=(jax.ShapeD...  8.49 us

profile of v1, /device:TPU:0, one launch (start us, length us, event | category | flops | bytes accessed | tf_op | source)
XLA Modules:
  0.0 35.7 jit_solution(6743097399049608952)
XLA Ops:
  1.3 26.0 %exchange.1 = (bf16[4,2,128,512]{3,2,1,0:T(8,128)(2,1)}, s32[8,1,128]{2,1,0:T(1,128)}) custom-call(s32[1]{0:T(128)S(6)} %copy.9.counts_ref, s32[8]{0:T(128)} %hops_ref.3, s32[8]{0:T(128)} %pos_ref.3, bf16[8,2,128,512]{3,2,1,0:T(8,128)(2,1)} %kv_ref.3), custom_call_target="tpu_custom_call" | custom-call | tf_op jit(solution)/shard_map/exchange/pallas_call | solution.py:82
  27.2 8.5 %decode.1 = (bf16[8,2,128,512]{3,2,1,0:T(8,128)(2,1)}, bf16[8,2,4096]{2,1,0:T(2,128)(2,1)}, s32[8]{0:T(128)}) custom-call(s32[1]{0:T(128)S(6)} %copy.9.counts_ref, s32[8]{0:T(128)} %hops_ref.3, s32[8]{0:T(128)} %pos_ref.3, s32[8,1,128]{2,1,0:T(1,128)} %get-tuple-element.5.table_ref, bf16[8,2,128,512]{3,2,1,0:T(8,128)(2,1)} %kv_ref.3, ...), custom_call_target="tpu_custom_call" | custom-call | tf_op jit(solution)/shard_map/decode/pallas_call | solution.py:198

commit v2 on v1

v2 whole, which is shorter than its diff:
```python
import functools

import jax
import jax.numpy as jnp
from jax import lax
from jax.experimental import pallas as pl
from jax.experimental.pallas import tpu as pltpu
from jax.sharding import PartitionSpec as P

HEAD_DIM = 128
SINK = 4
OFFSETS = (-2, -1, 1, 2)
PACK = 16


def attend(pair, fresh_of, keys_of, values_of, target, q_rows, o_rows):
    heads = pair.shape[-1] // HEAD_DIM
    q = pair.astype(jnp.float32)
    for h in range(heads):
        q_rows[2 * h:2 * h + 2] = q[:, h * HEAD_DIM:(h + 1) * HEAD_DIM]
    fresh = [fresh_of(c).astype(jnp.float32) for c in range(2)]
    kv_heads = fresh[0].shape[-1] // HEAD_DIM
    rows = 2 * heads // kv_heads
    for g in range(kv_heads):
        lanes = slice(g * HEAD_DIM, (g + 1) * HEAD_DIM)
        query = q_rows[g * rows:(g + 1) * rows]
        keys, values = keys_of(lanes), values_of(lanes)
        column = lax.broadcasted_iota(jnp.int32, (rows, keys.shape[0]), 1)
        second = lax.rem(lax.broadcasted_iota(jnp.int32, (rows, keys.shape[0]), 0), 2) == 1
        hits = [column == target[0], (column == target[1]) & second]
        scores = lax.dot_general(query.astype(jnp.bfloat16), keys, (((1,), (1,)), ((), ())),
                                 preferred_element_type=jnp.float32)
        for t in range(2):
            now = jnp.sum(query * fresh[0][t:t + 1, lanes], axis=1, keepdims=True)
            scores = jnp.where(hits[t], now, scores)
        scores = scores * HEAD_DIM ** -0.5
        raised = jnp.exp(scores - jnp.max(scores, axis=1, keepdims=True))
        weights = (raised / jnp.sum(raised, axis=1, keepdims=True)).astype(jnp.bfloat16)
        wide = weights.astype(jnp.float32)
        kept = jnp.where(hits[0] | hits[1], 0.0, wide).astype(jnp.bfloat16)
        mixed = lax.dot_general(kept, values, (((1,), (0,)), ((), ())),
                                preferred_element_type=jnp.float32)
        for t in range(2):
            share = jnp.sum(jnp.where(hits[t], wide, 0.0), axis=1, keepdims=True)
            mixed = mixed + share * fresh[1][t:t + 1, lanes]
        o_rows[g * rows:(g + 1) * rows] = mixed


def put_heads(ref, j, o_rows):
    for h in range(ref.shape[-1] // HEAD_DIM):
        ref[j, :, h * HEAD_DIM:(h + 1) * HEAD_DIM] = o_rows[2 * h:2 * h + 2].astype(ref.dtype)


def exchange_kernel(n, counts_ref, hops_ref, pos_ref, kv_hbm, q_ref, fresh_ref, arrived_ref, table_ref, local_ref,
                    kv_ref, staged, meta, q_rows, o_rows, dest, load_sem, send_sem, recv_sem, meta_send, meta_recv,
                    own_sem):
    me = lax.axis_index("grp")
    slots = kv_ref.shape[0]
    barrier = pltpu.get_barrier_semaphore()

    @pl.loop(1, n)
    def _(k):
        pl.semaphore_signal(barrier, inc=1, device_id={"grp": lax.rem(me + k, n)})

    load = pltpu.make_async_copy(kv_hbm, kv_ref, load_sem)
    load.start()
    live = counts_ref[0]
    stay = jnp.int32(0)
    picked = [jnp.int32(0) for _ in OFFSETS]
    position = [jnp.int32(-1) for _ in OFFSETS]
    for s in range(slots):
        hop = jnp.where(s < live, hops_ref[s], 0)
        dest[s] = stay
        stay = stay + jnp.where((s < live) & (hop == 0), 1, 0)
        for i, offset in enumerate(OFFSETS):
            hit = hop == offset
            picked[i] = jnp.where(hit, s, picked[i])
            position[i] = jnp.where(hit, pos_ref[s], position[i])
    lane = lax.broadcasted_iota(jnp.int32, (1, 128), 1)
    row = jnp.where(lane == 0, stay, 0)
    for i in range(len(OFFSETS)):
        row = jnp.where(lane == 1 + i, position[i], row)
    meta[...] = row
    load.wait()
    for i in range(len(OFFSETS)):
        staged[i] = kv_ref[picked[i]]

    pl.semaphore_wait(barrier, n - 1)

    def meta_copy(k):
        return pltpu.make_async_remote_copy(
            src_ref=meta, dst_ref=table_ref.at[me], send_sem=meta_send.at[k],
            recv_sem=meta_recv.at[k], device_id={"grp": lax.rem(me + k, n)})

    copies = []
    for i, offset in enumerate(OFFSETS):
        copies.append(pltpu.make_async_remote_copy(
            src_ref=staged.at[i], dst_ref=arrived_ref.at[i], send_sem=send_sem.at[i],
            recv_sem=recv_sem.at[i], device_id={"grp": lax.rem(me + offset + n, n)}))

    @pl.loop(1, n)
    def _(k):
        meta_copy(k).start()

    for i in (0, 3, 1, 2):
        copies[i].start()
    own = pltpu.make_async_copy(meta, table_ref.at[me], own_sem)
    own.start()
    window = kv_ref.shape[2] - SINK

    @pl.loop(0, slots)
    def _(s):
        at = jnp.minimum(dest[s], slots - 1)
        position = pos_ref[s]
        target = [SINK + lax.rem(position + t, window) for t in range(2)]
        attend(q_ref[at], lambda c: fresh_ref[at, c], lambda lanes: kv_ref[s, 0, :, lanes],
               lambda lanes: kv_ref[s, 1, :, lanes], target, q_rows, o_rows)
        put_heads(local_ref, s, o_rows)

    own.wait()

    @pl.loop(1, n)
    def _(k):
        meta_copy(k).wait()

    for copy in copies:
        copy.wait()


def exchange(n, counts, hops, pos, kv, queries, fresh):
    many = len(OFFSETS)
    heads = queries.shape[-1] // HEAD_DIM
    smem = pl.BlockSpec(memory_space=pltpu.SMEM)
    vmem = pl.BlockSpec(memory_space=pltpu.VMEM)
    hbm = pl.BlockSpec(memory_space=pl.ANY)
    dma = pltpu.SemaphoreType.DMA
    return pl.pallas_call(
        functools.partial(exchange_kernel, n),
        out_shape=(jax.ShapeDtypeStruct((many,) + kv.shape[1:], kv.dtype),
                   jax.ShapeDtypeStruct((n, 1, 128), jnp.int32),
                   jax.ShapeDtypeStruct(queries.shape, queries.dtype)),
        in_specs=[smem, smem, smem, hbm, vmem, vmem],
        out_specs=(hbm, hbm, vmem),
        scratch_shapes=[pltpu.VMEM(kv.shape, kv.dtype),
                        pltpu.VMEM((many,) + kv.shape[1:], kv.dtype),
                        pltpu.VMEM((1, 128), jnp.int32),
                        pltpu.VMEM((2 * heads, HEAD_DIM), jnp.float32),
                        pltpu.VMEM((2 * heads, HEAD_DIM), jnp.float32),
                        pltpu.SMEM((kv.shape[0],), jnp.int32),
                        dma(()), dma((many,)), dma((many,)), dma((n,)), dma((n,)), dma(())],
        compiler_params=pltpu.CompilerParams(collective_id=0, has_side_effects=True),
        name="exchange",
    )(counts, hops, pos, kv, queries, fresh)


def decode_kernel(n, counts_ref, hops_ref, pos_ref, table_ref, kv_ref, arrived_ref, q_ref, fresh_ref, local_ref,
                  out_ref, heads_ref, served_ref,
                  buf, raw, zeros, q_rows, o_rows, place_pos, in_sem, raw_sem, out_sem):
    me = lax.axis_index("grp")
    slots, _, cache_len, width = kv_ref.shape
    window = cache_len - SINK

    live = counts_ref[0]
    filled = jnp.int32(0)
    for s in range(slots):
        stays = (s < live) & (hops_ref[s] == 0)

        @pl.when(stays)
        def _(s=s, at=filled):
            place_pos[at] = pos_ref[s]
            pltpu.make_async_copy(kv_ref.at[s], buf.at[at], in_sem.at[at]).start()
            heads_ref[at] = local_ref[s]

        filled = filled + jnp.where(stays, 1, 0)
    stayed = filled
    for i, offset in enumerate(OFFSETS):
        position = table_ref[lax.rem(me - offset + n, n), 0, 1 + i]
        present = position >= 0

        @pl.when(present)
        def _(i=i, at=filled, position=position):
            place_pos[at] = position
            pltpu.make_async_copy(arrived_ref.at[i], buf.at[at], in_sem.at[at]).start()
            pltpu.make_async_copy(arrived_ref.at[i], raw.at[at - stayed], raw_sem.at[at - stayed]).start()

        filled = filled + jnp.where(present, 1, 0)

    zeros[...] = jnp.zeros_like(zeros)

    @pl.loop(0, n)
    def _(g):
        total = table_ref[g, 0, 0]
        for i, offset in enumerate(OFFSETS):
            total = total + jnp.where(table_ref[lax.rem(g - offset + n, n), 0, 1 + i] >= 0, 1, 0)
        served_ref[g] = total

    @pl.loop(filled, slots)
    def _(j):
        heads_ref[j] = jnp.zeros(heads_ref.shape[1:], heads_ref.dtype)
        pltpu.make_async_copy(zeros, out_ref.at[j], out_sem.at[j]).start()

    sub = lax.broadcasted_iota(jnp.int32, (PACK, width), 0)

    @pl.loop(0, filled)
    def _(j):
        pltpu.make_async_copy(kv_ref.at[0], buf.at[j], in_sem.at[j]).wait()
        position = place_pos[j]
        target = [SINK + lax.rem(position + t, window) for t in range(2)]
        for c in range(2):
            fresh = fresh_ref[j, c].astype(jnp.float32)
            for t in range(2):
                base = pl.multiple_of((target[t] // PACK) * PACK, PACK)
                block = buf[j, c, pl.ds(base, PACK), :].astype(jnp.float32)
                hit = sub + base == target[t]
                buf[j, c, pl.ds(base, PACK), :] = jnp.where(hit, fresh[t:t + 1], block).astype(buf.dtype)
        pltpu.make_async_copy(buf.at[j], out_ref.at[j], out_sem.at[j]).start()

    @pl.loop(stayed, filled)
    def _(j):
        k = j - stayed
        pltpu.make_async_copy(arrived_ref.at[0], raw.at[k], raw_sem.at[k]).wait()
        position = place_pos[j]
        target = [SINK + lax.rem(position + t, window) for t in range(2)]
        attend(q_ref[j], lambda c: fresh_ref[j, c], lambda lanes: raw[k, 0, :, lanes],
               lambda lanes: raw[k, 1, :, lanes], target, q_rows, o_rows)
        put_heads(heads_ref, j, o_rows)

    @pl.loop(0, slots)
    def _(j):
        pltpu.make_async_copy(zeros, out_ref.at[j], out_sem.at[j]).wait()


def decode(n, counts, hops, pos, table, kv, arrived, queries, fresh, local):
    smem = pl.BlockSpec(memory_space=pltpu.SMEM)
    vmem = pl.BlockSpec(memory_space=pltpu.VMEM)
    hbm = pl.BlockSpec(memory_space=pl.ANY)
    dma = pltpu.SemaphoreType.DMA
    slots = kv.shape[0]
    heads = queries.shape[-1] // HEAD_DIM
    return pl.pallas_call(
        functools.partial(decode_kernel, n),
        out_shape=(jax.ShapeDtypeStruct(kv.shape, kv.dtype),
                   jax.ShapeDtypeStruct(queries.shape, queries.dtype),
                   jax.ShapeDtypeStruct((n,), jnp.int32)),
        in_specs=[smem, smem, smem, smem, hbm, hbm, vmem, vmem, vmem],
        out_specs=(hbm, vmem, smem),
        scratch_shapes=[pltpu.VMEM(kv.shape, kv.dtype),
                        pltpu.VMEM(arrived.shape, kv.dtype),
                        pltpu.VMEM(kv.shape[1:], kv.dtype),
                        pltpu.VMEM((2 * heads, HEAD_DIM), jnp.float32),
                        pltpu.VMEM((2 * heads, HEAD_DIM), jnp.float32),
                        pltpu.SMEM((slots,), jnp.int32),
                        dma((slots,)), dma((len(OFFSETS),)), dma((slots,))],
        name="decode",
    )(counts, hops, pos, table, kv, arrived, queries, fresh, local)


def solution(mesh):
    n = mesh.shape["grp"]

    def per_device(counts, hop_offsets, write_pos, kv_cache, queries, fresh_kv):
        arrived, table, local = exchange(n, counts, hop_offsets, write_pos, kv_cache, queries, fresh_kv)
        return decode(n, counts, hop_offsets, write_pos, table, kv_cache, arrived, queries, fresh_kv, local)

    return jax.shard_map(
        per_device,
        mesh=mesh,
        in_specs=(
            P(("rep", "grp")),
            P(("rep", "grp")),
            P(("rep", "grp")),
            P(("rep", "grp"), None, None, "tp"),
            P(("rep", "grp"), None, "tp"),
            P(("rep", "grp"), None, None, "tp"),
        ),
        out_specs=(P(("rep", "grp"), None, None, "tp"), P(("rep", "grp"), None, "tp"), P("rep")),
        check_vma=False,
    )
```

time: 35.9 us -> 33.8 us (0.942)
  Pallas kernels: 34.5 us -> 32.3 us
    pallas_call x1, Pallas kernels: 8.49 us -> 4.85 us  [decode(): pl.pallas_call(functools.partial(decode_kernel, n), out_shape=(jax.ShapeD...]
    pallas_call x1, Pallas kernels: 26 us -> 27.4 us  [exchange(): pl.pallas_call(functools.partial(exchange_kernel, n), out_shape=(jax.Shap...]
where the time goes in v2:
time: 33.8 us; the launch traced here: 33.5 us
  Pallas kernels  32.3 us (96%)
  between operations  1.28 us (4%)
    pallas_call x1, Pallas kernels, exchange(): pl.pallas_call(functools.partial(exchange_kernel, n), out_shape=(jax.Shap...  27.4 us
    pallas_call x1, Pallas kernels, decode(): pl.pallas_call(functools.partial(decode_kernel, n), out_shape=(jax.ShapeD...  4.85 us

profile of v2, /device:TPU:0, one launch (start us, length us, event | category | flops | bytes accessed | tf_op | source)
XLA Modules:
  0.0 33.5 jit_solution(716842905791830683)
XLA Ops:
  1.3 27.4 %exchange.1 = (bf16[4,2,128,512]{3,2,1,0:T(8,128)(2,1)}, s32[8,1,128]{2,1,0:T(1,128)}, bf16[8,2,4096]{2,1,0:T(2,128)(2,1)}) custom-call(s32[1]{0:T(128)S(6)} %copy.9.counts_ref, s32[8]{0:T(128)} %hops_ref.3, s32[8]{0:T(128)} %pos_ref.3, bf16[8,2,128,512]{3,2,1,0:T(8,128)(2,1)} %kv_ref.1, bf16[8,2,4096]{2,1,0:T(2,128)(2,1)} %q_ref.3, ...), custom_call_target="tpu_custom_call" | custom-call | tf_op jit(solution)/shard_map/exchange/pallas_call | solution.py:137
  28.7 4.8 %decode.1 = (bf16[8,2,128,512]{3,2,1,0:T(8,128)(2,1)}, bf16[8,2,4096]{2,1,0:T(2,128)(2,1)}, s32[8]{0:T(128)}) custom-call(s32[1]{0:T(128)S(6)} %copy.9.counts_ref, s32[8]{0:T(128)} %hops_ref.3, s32[8]{0:T(128)} %pos_ref.3, s32[8,1,128]{2,1,0:T(1,128)} %get-tuple-element.6.table_ref, bf16[8,2,128,512]{3,2,1,0:T(8,128)(2,1)} %kv_ref.1, ...), custom_call_target="tpu_custom_call" | custom-call | tf_op jit(solution)/shard_map/decode/pallas_call | solution.py:240

commit v3 on v2

--- a/solution.py
+++ b/solution.py
@@ -51,8 +51,8 @@
         ref[j, :, h * HEAD_DIM:(h + 1) * HEAD_DIM] = o_rows[2 * h:2 * h + 2].astype(ref.dtype)
 
 
-def exchange_kernel(n, counts_ref, hops_ref, pos_ref, kv_hbm, q_ref, fresh_ref, arrived_ref, table_ref, local_ref,
-                    kv_ref, staged, meta, q_rows, o_rows, dest, load_sem, send_sem, recv_sem, meta_send, meta_recv,
+def exchange_kernel(n, counts_ref, hops_ref, pos_ref, kv_hbm, q_hbm, fresh_hbm, arrived_ref, table_ref, local_ref,
+                    kv_ref, q_ref, fresh_ref, staged, meta, q_rows, o_rows, dest, load_sem, send_sem, recv_sem, meta_send, meta_recv,
                     own_sem):
     me = lax.axis_index("grp")
     slots = kv_ref.shape[0]
@@ -62,8 +62,12 @@
     def _(k):
         pl.semaphore_signal(barrier, inc=1, device_id={"grp": lax.rem(me + k, n)})
 
-    load = pltpu.make_async_copy(kv_hbm, kv_ref, load_sem)
+    load = pltpu.make_async_copy(kv_hbm, kv_ref, load_sem.at[0])
     load.start()
+    others = [pltpu.make_async_copy(q_hbm, q_ref, load_sem.at[1]),
+              pltpu.make_async_copy(fresh_hbm, fresh_ref, load_sem.at[2])]
+    for other in others:
+        other.start()
     live = counts_ref[0]
     stay = jnp.int32(0)
     picked = [jnp.int32(0) for _ in OFFSETS]
@@ -106,6 +110,8 @@
         copies[i].start()
     own = pltpu.make_async_copy(meta, table_ref.at[me], own_sem)
     own.start()
+    for other in others:
+        other.wait()
     window = kv_ref.shape[2] - SINK
 
     @pl.loop(0, slots)
@@ -139,15 +145,17 @@
         out_shape=(jax.ShapeDtypeStruct((many,) + kv.shape[1:], kv.dtype),
                    jax.ShapeDtypeStruct((n, 1, 128), jnp.int32),
                    jax.ShapeDtypeStruct(queries.shape, queries.dtype)),
-        in_specs=[smem, smem, smem, hbm, vmem, vmem],
+        in_specs=[smem, smem, smem, hbm, hbm, hbm],
         out_specs=(hbm, hbm, vmem),
         scratch_shapes=[pltpu.VMEM(kv.shape, kv.dtype),
+                        pltpu.VMEM(queries.shape, queries.dtype),
+                        pltpu.VMEM(fresh.shape, fresh.dtype),
                         pltpu.VMEM((many,) + kv.shape[1:], kv.dtype),
                         pltpu.VMEM((1, 128), jnp.int32),
                         pltpu.VMEM((2 * heads, HEAD_DIM), jnp.float32),
                         pltpu.VMEM((2 * heads, HEAD_DIM), jnp.float32),
                         pltpu.SMEM((kv.shape[0],), jnp.int32),
-                        dma(()), dma((many,)), dma((many,)), dma((n,)), dma((n,)), dma(())],
+                        dma((3,)), dma((many,)), dma((many,)), dma((n,)), dma((n,)), dma(())],
         compiler_params=pltpu.CompilerParams(collective_id=0, has_side_effects=True),
         name="exchange",
     )(counts, hops, pos, kv, queries, fresh)

time: 33.8 us -> 33.6 us (level)
  no operation moved by 1% of the time
where the time goes in v3:
time: 33.6 us; the launch traced here: 33.4 us
  Pallas kernels  32.1 us (96%)
  between operations  1.28 us (4%)
    pallas_call x1, Pallas kernels, exchange(): pl.pallas_call(functools.partial(exchange_kernel, n), out_shape=(jax.Shap...  27.2 us
    pallas_call x1, Pallas kernels, decode(): pl.pallas_call(functools.partial(decode_kernel, n), out_shape=(jax.ShapeD...  4.94 us

profile of v3, /device:TPU:0, one launch (start us, length us, event | category | flops | bytes accessed | tf_op | source)
XLA Modules:
  0.0 33.4 jit_solution(11149564375511903522)
XLA Ops:
  1.3 27.2 %exchange.1 = (bf16[4,2,128,512]{3,2,1,0:T(8,128)(2,1)}, s32[8,1,128]{2,1,0:T(1,128)}, bf16[8,2,4096]{2,1,0:T(2,128)(2,1)}) custom-call(s32[1]{0:T(128)S(6)} %copy.9.counts_ref, s32[8]{0:T(128)} %hops_ref.3, s32[8]{0:T(128)} %pos_ref.3, bf16[8,2,128,512]{3,2,1,0:T(8,128)(2,1)} %kv_ref.1, bf16[8,2,4096]{2,1,0:T(2,128)(2,1)} %q_ref.1, ...), custom_call_target="tpu_custom_call" | custom-call | tf_op jit(solution)/shard_map/exchange/pallas_call | solution.py:143
  28.5 4.9 %decode.1 = (bf16[8,2,128,512]{3,2,1,0:T(8,128)(2,1)}, bf16[8,2,4096]{2,1,0:T(2,128)(2,1)}, s32[8]{0:T(128)}) custom-call(s32[1]{0:T(128)S(6)} %copy.9.counts_ref, s32[8]{0:T(128)} %hops_ref.3, s32[8]{0:T(128)} %pos_ref.3, s32[8,1,128]{2,1,0:T(1,128)} %get-tuple-element.6.table_ref, bf16[8,2,128,512]{3,2,1,0:T(8,128)(2,1)} %kv_ref.1, ...), custom_call_target="tpu_custom_call" | custom-call | tf_op jit(solution)/shard_map/decode/pallas_call | solution.py:248
